TPU v7x, 32 devices: a whole 2x2x4 slice. The times are simulated.
32 devices in a mesh: batch: 2 (over y), row: 4 (over x, core), col: 4 (over z).
Axes of the slice: x: 2, y: 2, z: 4, core: 2. Of those that a mesh axis runs over, the one named last changes fastest.
Arguments:
- patches: bfloat16 [2, 4096, 1280], P('batch', 'col', 'row'), may hold values from -6 to 6
- qkv_weight: bfloat16 [1280, 3, 1280], P('row', None, 'col'), may hold values from -0.15625 to 0.15625
- qv_bias: float32 [2, 1280], P(None, 'col'), may hold values from -0.6 to 0.6
- proj_weight: bfloat16 [1280, 1280], P('col', 'row'), may hold values from -2.5 to 2.5
- proj_bias: float32 [1280], P('row'), may hold values from -1.2 to 1.2
- norm1_gain: float32 [1280], P('row'), may hold values from 0.5 to 1.5
- norm1_shift: float32 [1280], P('row'), may hold values from -1.2 to 1.2
- norm2_gain: float32 [1280], P('row'), may hold values from 0.5 to 1.5
- norm2_shift: float32 [1280], P('row'), may hold values from -1.2 to 1.2
- fc1_weight: bfloat16 [1280, 5120], P('row', 'col'), may hold values from -0.15625 to 0.15625
- fc1_bias: float32 [5120], P('col'), may hold values from -1.2 to 1.2
- fc2_weight: bfloat16 [5120, 1280], P('col', 'row'), may hold values from -0.078125 to 0.078125
- fc2_bias: float32 [1280], P('row'), may hold values from -1.2 to 1.2
- height_table: bfloat16 [127, 80], replicated, may hold values from -0.625 to 0.625
- width_table: bfloat16 [127, 80], replicated, may hold values from -0.625 to 0.625
- out_grad: bfloat16 [2, 4096, 1280], P('batch', 'col', 'row'), may hold values from -6 to 6
Outputs:
- block_out: bfloat16 [2, 4096, 1280], P('batch', 'col', 'row')
- patches_grad: float32 [2, 4096, 1280], P('batch', 'col', 'row')
- qkv_weight_grad: float32 [1280, 3, 1280], P('row', None, 'col')
- qv_bias_grad: float32 [2, 1280], P(None, 'col')
- proj_weight_grad: float32 [1280, 1280], P('col', 'row')
- proj_bias_grad: float32 [1280], P('row')
- norm1_gain_grad: float32 [1280], P('row')
- norm1_shift_grad: float32 [1280], P('row')
- norm2_gain_grad: float32 [1280], P('row')
- norm2_shift_grad: float32 [1280], P('row')
- fc1_weight_grad: float32 [1280, 5120], P('row', 'col')
- fc1_bias_grad: float32 [5120], P('col')
- fc2_weight_grad: float32 [5120, 1280], P('col', 'row')
- fc2_bias_grad: float32 [1280], P('row')
- height_table_grad: float32 [127, 80], replicated
- width_table_grad: float32 [127, 80], replicated
All inputs are finite; a program needn't handle non-finite values.
Results may differ from a plain program's by a relative error of at most 0.012.
Values may be sent and summed in bfloat16 or wider, within the bound.
A program may use at most 256 MiB of HBM per device.

v0:
```python
from functools import partial
import jax
import jax.numpy as jnp
from jax import lax
from jax.sharding import PartitionSpec as P

D = 1280
HEAD_DIM = 80
GRID = 64
EPSILON = 1e-06
HIGHEST = lax.Precision.HIGHEST


def feature_sums(first, second):
    return lax.psum((first, second), "row")


def rows_over_col(values):
    return lax.all_gather(values, "col", axis=0, tiled=True)


def rows_over_row(values):
    return lax.all_gather(values, "row", axis=0, tiled=True)


def sum_over_row(values):
    return lax.psum_scatter(values, "row", scatter_dimension=0, tiled=True)


def sum_over_col(values):
    return lax.psum_scatter(values, "col", scatter_dimension=0, tiled=True)


def gather_key_value(key_local, value_local):
    couple = jnp.stack([key_local, value_local], 1).astype(jnp.bfloat16)
    couple_full = lax.all_gather(couple, "row", axis=0, tiled=True)
    return (couple_full[:, 0], couple_full[:, 1])


def normalize(values, norm_gain, norm_shift, model_width):
    first, second = feature_sums(jnp.sum(values, -1), jnp.sum(values * values, -1))
    center = first / model_width
    inv_scale = lax.rsqrt(second / model_width - center * center + EPSILON)
    scaled = (values - center[:, None]) * inv_scale[:, None]
    return (scaled, inv_scale, (scaled * norm_gain + norm_shift).astype(jnp.bfloat16))


def normalize_back(grad_in, scaled, inv_scale, norm_gain, model_width):
    scaled_grad = grad_in * norm_gain
    first, second = feature_sums(jnp.sum(scaled_grad, -1), jnp.sum(scaled_grad * scaled, -1))
    return inv_scale[:, None] * (
        scaled_grad - first[:, None] / model_width - scaled * (second[:, None] / model_width)
    )


def select_table(row_count, col_count, offset, grid_side):
    shape = (row_count, col_count, 2 * grid_side - 1)
    first = lax.broadcasted_iota(jnp.int32, shape, 0) + offset
    second = lax.broadcasted_iota(jnp.int32, shape, 1)
    third = lax.broadcasted_iota(jnp.int32, shape, 2)
    return (first - second + grid_side - 1 == third).astype(jnp.bfloat16)


def head_scores(query_one, key_one, row_select, col_select, score_scale, grid_side):
    query_lines = query_one.shape[0] // grid_side
    query_grid = query_one.reshape(query_lines, grid_side, query_one.shape[1])
    rel_rows = jnp.einsum(
        "hwc,hkc->hwk", query_grid, row_select, preferred_element_type=jnp.float32
    )
    rel_cols = jnp.einsum(
        "hwc,wkc->hwk", query_grid, col_select, preferred_element_type=jnp.float32
    )
    position = (rel_rows[:, :, :, None] + rel_cols[:, :, None, :]).reshape(
        query_one.shape[0], grid_side * grid_side
    )
    raw = jnp.einsum("qc,kc->qk", query_one, key_one, preferred_element_type=jnp.float32)
    return raw * score_scale + position


def shards(
    patches,
    qkv_weight,
    qv_bias,
    proj_weight,
    proj_bias,
    norm1_gain,
    norm1_shift,
    norm2_gain,
    norm2_shift,
    fc1_weight,
    fc1_bias,
    fc2_weight,
    fc2_bias,
    height_table,
    width_table,
    out_grad,
):
    grid_side = GRID
    model_width = D
    head_size = HEAD_DIM
    score_scale = head_size ** (-0.5)
    local_cols = qkv_weight.shape[2]
    head_count = local_cols // head_size
    image_tokens = grid_side * grid_side
    query_rows = image_tokens // lax.axis_size("row")
    query_lines = query_rows // grid_side
    residual = patches[0].astype(jnp.float32)
    scaled1, inv_scale1, normed1 = normalize(residual, norm1_gain, norm1_shift, model_width)
    gathered1 = rows_over_col(normed1)
    partial_qkv = jnp.einsum(
        "lf,fkh->lkh", gathered1, qkv_weight, preferred_element_type=jnp.float32
    )
    local_qkv = sum_over_row(partial_qkv)
    queries = local_qkv[:, 0] + qv_bias[0]
    key_full, value_full = gather_key_value(local_qkv[:, 1], local_qkv[:, 2] + qv_bias[1])
    queries = queries.astype(jnp.bfloat16)
    row_onehot = select_table(
        query_lines, grid_side, lax.axis_index("row") * query_lines, grid_side
    )
    col_onehot = select_table(grid_side, grid_side, 0, grid_side)
    row_select = jnp.einsum(
        "ijd,dc->ijc", row_onehot, height_table, preferred_element_type=jnp.float32
    ).astype(jnp.bfloat16)
    col_select = jnp.einsum(
        "ijd,dc->ijc", col_onehot, width_table, preferred_element_type=jnp.float32
    ).astype(jnp.bfloat16)

    def split_heads(values):
        return values.reshape(values.shape[0], head_count, head_size).transpose(1, 0, 2)

    def join_heads(values):
        return values.transpose(1, 0, 2).reshape(values.shape[1], head_count * head_size)

    query_heads = split_heads(queries)
    key_heads = split_heads(key_full)
    value_heads = split_heads(value_full)

    def attend(operands):
        query_one, key_one, value_one = operands
        scores = head_scores(query_one, key_one, row_select, col_select, score_scale, grid_side)
        row_max = jnp.max(scores, -1, keepdims=True)
        raw_weights = jnp.exp(scores - row_max)
        row_total = jnp.sum(raw_weights, -1, keepdims=True)
        weights = (raw_weights / row_total).astype(jnp.bfloat16)
        result = jnp.dot(weights, value_one, preferred_element_type=jnp.float32).astype(
            jnp.bfloat16
        )
        return (result, (row_max + jnp.log(row_total))[:, 0])

    attended, log_total = lax.map(attend, (query_heads, key_heads, value_heads))
    merged = join_heads(attended)
    gathered_attn = rows_over_row(merged)
    projected = sum_over_col(
        jnp.dot(gathered_attn, proj_weight, preferred_element_type=jnp.float32)
    )
    middle = residual + (projected + proj_bias)
    scaled2, inv_scale2, normed2 = normalize(middle, norm2_gain, norm2_shift, model_width)
    gathered2 = rows_over_col(normed2)
    preact = (
        sum_over_row(jnp.dot(gathered2, fc1_weight, preferred_element_type=jnp.float32)) + fc1_bias
    )
    activated = jax.nn.gelu(preact, approximate=False).astype(jnp.bfloat16)
    gathered_act = rows_over_row(activated)
    lowered = sum_over_col(jnp.dot(gathered_act, fc2_weight, preferred_element_type=jnp.float32))
    final = middle + (lowered + fc2_bias)
    cotangent = out_grad[0]
    cot_all = rows_over_col(cotangent)
    fc2_grad, fc2_bias_grad = (
        jnp.einsum("lh,lf->hf", gathered_act, cot_all, preferred_element_type=jnp.float32),
        jnp.sum(cot_all, 0, dtype=jnp.float32),
    )
    act_grad = sum_over_row(
        jnp.einsum("lf,hf->lh", cot_all, fc2_weight, preferred_element_type=jnp.float32)
    )
    gelu_fn = partial(jax.nn.gelu, approximate=False)
    unused, gelu_back = jax.vjp(gelu_fn, preact)
    preact_grad = gelu_back(act_grad)[0].astype(jnp.bfloat16)
    preact_all = rows_over_row(preact_grad)
    fc1_grad, fc1_bias_grad = (
        jnp.einsum("lf,lh->fh", gathered2, preact_all, preferred_element_type=jnp.float32),
        jnp.sum(preact_all, 0, dtype=jnp.float32),
    )
    normed2_grad = sum_over_col(
        jnp.einsum("lh,fh->lf", preact_all, fc1_weight, preferred_element_type=jnp.float32)
    )
    gain2_part = jnp.sum(normed2_grad * scaled2, 0)
    shift2_part = jnp.sum(normed2_grad, 0)
    middle_grad = cotangent.astype(jnp.float32) + normalize_back(
        normed2_grad, scaled2, inv_scale2, norm2_gain, model_width
    )
    branch_grad = middle_grad.astype(jnp.bfloat16)
    branch_all = rows_over_col(branch_grad)
    proj_grad, proj_bias_grad = (
        jnp.einsum("lh,lf->hf", gathered_attn, branch_all, preferred_element_type=jnp.float32),
        jnp.sum(branch_all, 0, dtype=jnp.float32),
    )
    merged_grad = sum_over_row(
        jnp.einsum("lf,hf->lh", branch_all, proj_weight, preferred_element_type=jnp.float32)
    ).astype(jnp.bfloat16)
    merged_grad_heads = split_heads(merged_grad)

    def attend_back(operands):
        query_one, key_one, value_one, grad_one, total_one = operands
        scores = head_scores(query_one, key_one, row_select, col_select, score_scale, grid_side)
        weights = jnp.exp(scores - total_one[:, None])
        weight_grad = jnp.einsum(
            "qc,kc->qk", grad_one, value_one, preferred_element_type=jnp.float32
        )
        row_inner = jnp.sum(weights * weight_grad, -1, keepdims=True)
        score_grad = (weights * (weight_grad - row_inner)).astype(jnp.bfloat16)
        value_part = jnp.einsum(
            "qk,qc->kc", weights.astype(jnp.bfloat16), grad_one, preferred_element_type=jnp.float32
        )
        key_part = (
            jnp.einsum("qk,qc->kc", score_grad, query_one, preferred_element_type=jnp.float32)
            * score_scale
        )
        query_part = jnp.dot(score_grad, key_one, preferred_element_type=jnp.float32) * score_scale
        grid_form = score_grad.astype(jnp.float32).reshape(
            query_lines, grid_side, grid_side, grid_side
        )
        row_grad = jnp.sum(grid_form, 3)
        col_grad = jnp.sum(grid_form, 2)
        query_grid = query_one.astype(jnp.float32).reshape(query_lines, grid_side, head_size)
        from_rows = jnp.einsum(
            "hwk,hkc->hwc", row_grad, row_select.astype(jnp.float32), precision=HIGHEST
        )
        from_cols = jnp.einsum(
            "hwk,wkc->hwc", col_grad, col_select.astype(jnp.float32), precision=HIGHEST
        )
        query_part = query_part + (from_rows + from_cols).reshape(query_rows, head_size)
        row_select_grad = jnp.einsum("hwk,hwc->hkc", row_grad, query_grid, precision=HIGHEST)
        col_select_grad = jnp.einsum("hwk,hwc->wkc", col_grad, query_grid, precision=HIGHEST)
        return (query_part, key_part, value_part, row_select_grad, col_select_grad)

    query_parts, key_parts, value_parts, row_sel_grads, col_sel_grads = lax.map(
        attend_back, (query_heads, key_heads, value_heads, merged_grad_heads, log_total)
    )
    kv_grad = sum_over_row(jnp.stack([join_heads(key_parts), join_heads(value_parts)], 1)).astype(
        jnp.bfloat16
    )
    query_grad = join_heads(query_parts).astype(jnp.bfloat16)
    qkv_grad_local = jnp.concatenate([query_grad[:, None], kv_grad], 1)
    qkv_all = rows_over_row(qkv_grad_local)
    qkv_grad, qv_bias_grad = (
        jnp.einsum("lf,lkh->fkh", gathered1, qkv_all, preferred_element_type=jnp.float32),
        jnp.stack(
            [
                jnp.sum(qkv_all[:, 0], 0, dtype=jnp.float32),
                jnp.sum(qkv_all[:, 2], 0, dtype=jnp.float32),
            ],
            0,
        ),
    )
    normed1_grad = sum_over_col(
        jnp.einsum("lkh,fkh->lf", qkv_all, qkv_weight, preferred_element_type=jnp.float32)
    )
    gain1_part = jnp.sum(normed1_grad * scaled1, 0)
    shift1_part = jnp.sum(normed1_grad, 0)
    input_grad = middle_grad + normalize_back(
        normed1_grad, scaled1, inv_scale1, norm1_gain, model_width
    )
    height_part = jnp.einsum(
        "ijd,ijc->dc", row_onehot.astype(jnp.float32), jnp.sum(row_sel_grads, 0), precision=HIGHEST
    )
    width_part = jnp.einsum(
        "ijd,ijc->dc", col_onehot.astype(jnp.float32), jnp.sum(col_sel_grads, 0), precision=HIGHEST
    )
    gain1_grad, shift1_grad, gain2_grad, shift2_grad = lax.psum(
        (gain1_part, shift1_part, gain2_part, shift2_part), ("batch", "col")
    )
    height_grad, width_grad = lax.psum((height_part, width_part), ("batch", "row", "col"))
    (
        qkv_grad,
        qv_bias_grad,
        proj_grad,
        proj_bias_grad,
        fc1_grad,
        fc1_bias_grad,
        fc2_grad,
        fc2_bias_grad,
    ) = (
        lax.psum(qkv_grad.astype(jnp.bfloat16), "batch").astype(jnp.float32),
        lax.psum(qv_bias_grad.astype(jnp.bfloat16), "batch").astype(jnp.float32),
        lax.psum(proj_grad.astype(jnp.bfloat16), "batch").astype(jnp.float32),
        lax.psum(proj_bias_grad.astype(jnp.bfloat16), "batch").astype(jnp.float32),
        lax.psum(fc1_grad.astype(jnp.bfloat16), "batch").astype(jnp.float32),
        lax.psum(fc1_bias_grad.astype(jnp.bfloat16), "batch").astype(jnp.float32),
        lax.psum(fc2_grad.astype(jnp.bfloat16), "batch").astype(jnp.float32),
        lax.psum(fc2_bias_grad.astype(jnp.bfloat16), "batch").astype(jnp.float32),
    )
    return (
        final[None].astype(jnp.bfloat16),
        input_grad[None],
        qkv_grad,
        qv_bias_grad,
        proj_grad,
        proj_bias_grad,
        gain1_grad,
        shift1_grad,
        gain2_grad,
        shift2_grad,
        fc1_grad,
        fc1_bias_grad,
        fc2_grad,
        fc2_bias_grad,
        height_grad,
        width_grad,
    )


def solution(mesh):
    in_specs = (
        P("batch", "col", "row"),
        P("row", None, "col"),
        P(None, "col"),
        P("col", "row"),
        P("row"),
        P("row"),
        P("row"),
        P("row"),
        P("row"),
        P("row", "col"),
        P("col"),
        P("col", "row"),
        P("row"),
        P(),
        P(),
        P("batch", "col", "row"),
    )
    out_specs = (
        P("batch", "col", "row"),
        P("batch", "col", "row"),
        P("row", None, "col"),
        P(None, "col"),
        P("col", "row"),
        P("row"),
        P("row"),
        P("row"),
        P("row"),
        P("row"),
        P("row", "col"),
        P("col"),
        P("col", "row"),
        P("row"),
        P(),
        P(),
    )
    return jax.shard_map(shards, mesh=mesh, in_specs=in_specs, out_specs=out_specs, check_vma=False)
```

profile of v0, /device:TPU:8, one launch (start us, length us, event | category | flops | bytes accessed | tf_op | source)
XLA Modules:
  0.0 2642.6 jit_solution(13296211281150519857)
XLA Ops:
  19.7 53.3 %all-gather.11.cloned.1.call-done = bf16[4096,320]{0,1:T(8,128)(2,1)} async-done(((bf16[1024,320]{0,1:T(8,128)(2,1)}), bf16[4096,320]{0,1:T(8,128)(2,1)}) %all-gather.11.cloned.1.call-update) | async-done | bytes 2621456 | tf_op jit(solution)/shard_map/all_gather | solution.py:19
  85.4 119.9 %reduce-scatter.10.cloned.1.call-done = f32[1024,3,320]{0,2,1:T(8,128)} async-done(((f32[4096,3,320]{0,2,1:T(8,128)}), f32[1024,3,320]{0,2,1:T(8,128)}) %reduce-scatter.10.cloned.1.call-update) | async-done | bytes 3932176 | tf_op jit(solution)/shard_map/reduce_scatter | solution.py:27
  218.2 33.4 %all-gather.13.cloned.1.call-done = bf16[4096,2,320]{0,2,1:T(8,128)(2,1)} async-done(((bf16[1024,2,320]{0,2,1:T(8,128)(2,1)}), bf16[4096,2,320]{0,2,1:T(8,128)(2,1)}) %all-gather.13.cloned.1.call-update) | async-done | bytes 5242896 | tf_op jit(solution)/shard_map/all_gather | solution.py:36
  268.2 293.5 %while.30 = (s32[]{:T(128)}, bf16[4,1024,80]{1,2,0:T(8,128)(2,1)S(1)}, f32[4,1024]{1,0:T(4,128)}, bf16[4,1024,80]{2,1,0:T(8,128)(2,1)}, bf16[4,4096,80]{2,1,0:T(...) while((s32[]{:T(128)}, ...), condition=%wide.region_8.9_spmd, body=%wide.region_5.8_spmd.sunk | while | flops 1400978432 | bytes 123054200 | solution.py:150
  281.7 27.9 %add.329 = f32[1024,4096]{1,0:T(8,128)} reshape(f32[16,64,64,64]{3,2,1,0:T(8,128)} %broadcast_add_fusion.4) | data formatting | bytes 33554432 | tf_op jit(solution)/shard_map/while/body/eval_jaxpr/add | solution.py:73
  309.6 14.6 fusion.193
  355.1 27.9 %add.329 = f32[1024,4096]{1,0:T(8,128)} reshape(f32[16,64,64,64]{3,2,1,0:T(8,128)} %broadcast_add_fusion.4) | data formatting | bytes 33554432 | tf_op jit(solution)/shard_map/while/body/eval_jaxpr/add | solution.py:73
  383.0 14.6 fusion.193
  428.4 27.9 %add.329 = f32[1024,4096]{1,0:T(8,128)} reshape(f32[16,64,64,64]{3,2,1,0:T(8,128)} %broadcast_add_fusion.4) | data formatting | bytes 33554432 | tf_op jit(solution)/shard_map/while/body/eval_jaxpr/add | solution.py:73
  456.3 14.6 fusion.193
  501.8 27.9 %add.329 = f32[1024,4096]{1,0:T(8,128)} reshape(f32[16,64,64,64]{3,2,1,0:T(8,128)} %broadcast_add_fusion.4) | data formatting | bytes 33554432 | tf_op jit(solution)/shard_map/while/body/eval_jaxpr/add | solution.py:73
  529.7 14.6 fusion.193
  562.8 25.5 all-gather.15.cloned.1.call-done
  594.5 93.3 %reduce-scatter.12.cloned.1.call-done = f32[1024,320]{0,1:T(8,128)} async-done(((f32[4096,320]{0,1:T(8,128)}), f32[1024,320]{0,1:T(8,128)}) %reduce-scatter.12.cloned.1.call-update) | async-done | bytes 1310736 | tf_op jit(solution)/shard_map/reduce_scatter | solution.py:31
  700.1 42.7 %all-gather.27.cloned.1.call-done = bf16[1,4096,320]{1,2,0:T(8,128)(2,1)} async-done(((bf16[1,1024,320]{1,2,0:T(8,128)(2,1)}), bf16[1,4096,320]{1,2,0:T(8,128)(2,1)}) %all-gather.27.cloned.1.call-update) | async-done | bytes 2621456 | tf_op jit(solution)/shard_map/all_gather | solution.py:19
  754.6 43.9 %all-gather.17.cloned.1.call-done = bf16[4096,320]{0,1:T(8,128)(2,1)} async-done(((bf16[1024,320]{0,1:T(8,128)(2,1)}), bf16[4096,320]{0,1:T(8,128)(2,1)}) %all-gather.17.cloned.1.call-update) | async-done | bytes 2621456 | tf_op jit(solution)/shard_map/all_gather | solution.py:19
  812.8 142.1 %reduce-scatter.18.cloned.1.call-done = f32[1024,1280]{1,0:T(8,128)} async-done(((f32[4096,1280]{1,0:T(8,128)}), f32[1024,1280]{1,0:T(8,128)}) %reduce-scatter.18.cloned.1.call-update) | async-done | bytes 5242896 | tf_op jit(solution)/shard_map/reduce_scatter | solution.py:27
  954.9 155.9 %reduce-scatter.14.cloned.1.call-done = f32[1024,1280]{1,0:T(8,128)} async-done(((f32[4096,1280]{1,0:T(8,128)}), f32[1024,1280]{1,0:T(8,128)}) %reduce-scatter.14.cloned.1.call-update) | async-done | bytes 5242896 | tf_op jit(solution)/shard_map/reduce_scatter | solution.py:27
  1110.8 15.3 add_convert_fusion
  1126.2 70.3 %all-gather.21.cloned.1.call-done = bf16[4096,1280]{1,0:T(8,128)(2,1)} async-done(((bf16[1024,1280]{1,0:T(8,128)(2,1)}), bf16[4096,1280]{1,0:T(8,128)(2,1)}) %all-gather.21.cloned.1.call-update) | async-done | bytes 10485776 | tf_op jit(solution)/shard_map/all_gather | solution.py:23
  1209.2 93.9 %reduce-scatter.20.cloned.1.call-done = f32[1024,320]{0,1:T(8,128)} async-done(((f32[4096,320]{0,1:T(8,128)}), f32[1024,320]{0,1:T(8,128)}) %reduce-scatter.20.cloned.1.call-update) | async-done | bytes 1310736 | tf_op jit(solution)/shard_map/reduce_scatter | solution.py:31
  1316.0 52.7 %all-gather.23.cloned.1.call-done = bf16[4096,320]{0,1:T(8,128)(2,1)} async-done(((bf16[1024,320]{0,1:T(8,128)(2,1)}), bf16[4096,320]{0,1:T(8,128)(2,1)}) %all-gather.23.cloned.1.call-update) | async-done | bytes 2621456 | tf_op jit(solution)/shard_map/all_gather | solution.py:19
  1374.4 52.1 %reduce-scatter.22.cloned.1.call-done = f32[1024,320]{0,1:T(8,128)} async-done(((f32[4096,320]{0,1:T(8,128)}), f32[1024,320]{0,1:T(8,128)}) %reduce-scatter.22.cloned.1.call-update) | async-done | bytes 1310736 | tf_op jit(solution)/shard_map/reduce_scatter | solution.py:27
  1429.1 574.5 %while.31 = (s32[]{:T(128)}, bf16[4,1024,80]{1,2,0:T(8,128)(2,1)}, f32[4,4096,80]{1,2,0:T(8,128)}, f32[4,4096,80]{1,2,0:T(8,128)}, f32[4,16,64,80]{3,2,1,0:T(8,1...) while((s32[]{:T(128)}, bf16[4,1024,80]{1,2,0:T(8,128)(2,1)}, ...), condition=%wide.region_27.28_spmd, body=%wide.region_23.27_spmd.sunk | while | flops 3678845952 | bytes 353068224 | solution.py:236
  1453.0 27.9 %add.336 = f32[1024,4096]{1,0:T(8,128)} reshape(f32[16,64,64,64]{3,2,1,0:T(8,128)} %broadcast_add_fusion.5) | data formatting | bytes 33554432 | tf_op jit(solution)/shard_map/while/body/eval_jaxpr/add | solution.py:73
  1480.9 16.5 multiply_reduce_fusion.7
  1520.3 24.0 reshape.157
  1544.3 15.4 fusion.218
  1596.6 27.9 %add.336 = f32[1024,4096]{1,0:T(8,128)} reshape(f32[16,64,64,64]{3,2,1,0:T(8,128)} %broadcast_add_fusion.5) | data formatting | bytes 33554432 | tf_op jit(solution)/shard_map/while/body/eval_jaxpr/add | solution.py:73
  1624.5 16.5 multiply_reduce_fusion.7
  1663.8 24.0 reshape.157
  1687.8 15.4 fusion.218
  1740.1 27.9 %add.336 = f32[1024,4096]{1,0:T(8,128)} reshape(f32[16,64,64,64]{3,2,1,0:T(8,128)} %broadcast_add_fusion.5) | data formatting | bytes 33554432 | tf_op jit(solution)/shard_map/while/body/eval_jaxpr/add | solution.py:73
  1768.0 16.5 multiply_reduce_fusion.7
  1807.3 24.0 reshape.157
  1831.3 15.4 fusion.218
  1883.5 27.9 %add.336 = f32[1024,4096]{1,0:T(8,128)} reshape(f32[16,64,64,64]{3,2,1,0:T(8,128)} %broadcast_add_fusion.5) | data formatting | bytes 33554432 | tf_op jit(solution)/shard_map/while/body/eval_jaxpr/add | solution.py:73
  1911.4 16.5 multiply_reduce_fusion.7
  1950.7 24.0 reshape.157
  1974.7 15.4 fusion.218
  2019.9 78.4 %reduce-scatter.24.cloned.1.call-done = f32[1024,2,320]{0,2,1:T(8,128)} async-done(((f32[4096,2,320]{0,2,1:T(8,128)}), f32[1024,2,320]{0,2,1:T(8,128)}) %reduce-scatter.24.cloned.1.call-update) | async-done | bytes 2621456 | tf_op jit(solution)/shard_map/reduce_scatter | solution.py:27
  2111.5 58.5 %all-gather.19.cloned.1.call-done = bf16[4096,1280]{1,0:T(8,128)(2,1)} async-done(((bf16[1024,1280]{1,0:T(8,128)(2,1)}), bf16[4096,1280]{1,0:T(8,128)(2,1)}) %all-gather.19.cloned.1.call-update) | async-done | bytes 10485776 | tf_op jit(solution)/shard_map/all_gather | solution.py:23
  2179.6 47.3 %all-gather.25.cloned.1.call-done = bf16[4096,3,320]{0,2,1:T(8,128)(2,1)} async-done(((bf16[1024,3,320]{0,2,1:T(8,128)(2,1)}), bf16[4096,3,320]{0,2,1:T(8,128)(2,1)}) %all-gather.25.cloned.1.call-update) | async-done | bytes 7864336 | tf_op jit(solution)/shard_map/all_gather | solution.py:23
  2285.6 25.0 all-reduce.13.cloned.1.call-done
  2318.5 88.2 %reduce-scatter.26.cloned.1.call-done = f32[1024,320]{0,1:T(8,128)} async-done(((f32[4096,320]{0,1:T(8,128)}), f32[1024,320]{0,1:T(8,128)}) %reduce-scatter.26.cloned.1.call-update) | async-done | bytes 1310736 | tf_op jit(solution)/shard_map/reduce_scatter | solution.py:31
  2415.5 87.7 %reduce-scatter.16.cloned.1.call-done = f32[1024,320]{0,1:T(8,128)} async-done(((f32[4096,320]{0,1:T(8,128)}), f32[1024,320]{0,1:T(8,128)}) %reduce-scatter.16.cloned.1.call-update) | async-done | bytes 1310736 | tf_op jit(solution)/shard_map/reduce_scatter | solution.py:31
  2507.6 19.1 all-reduce.1
  2526.7 106.0 %all-reduce.11.cloned.1.call-done = (f32[127,80]{0,1:T(8,128)}, f32[127,80]{0,1:T(8,128)}) async-done(((f32[127,80]{0,1:T(8,128)}, f32[127,80]{0,1:T(8,128)}), (f32[127,80]{0,1:T(8,128)}, f32[127,80]{0,1:T(8,128)})) %all-reduce.11.cloned.1.call-update) | async-done | bytes 81296 | tf_op jit(solution)/shard_map/psum | solution.py:272
  (322 shorter events, 617.2 us)
Async XLA Ops:
  7.2 791.3 %copy-start = (bf16[320,1280]{1,0:T(8,128)(2,1)S(1)}, bf16[320,1280]{1,0:T(8,128)(2,1)}, u32[]{:S(2)}) copy-start(bf16[320,1280]{1,0:T(8,128)(2,1)} %param.29) | copy-start | bytes 2457604
  7.2 65.8 %all-gather.11.cloned.1.call-start = ((), (), s32[]{:S(2)}) async-start(), calls=%async_computation.9 | async-start | bytes 3276800 | tf_op jit(solution)/shard_map/all_gather | solution.py:19
  19.7 185.7 %reduce-scatter.10.cloned.1.call-start = ((), (), s32[]{:S(2)}) async-start(), calls=%async_computation.10 | async-start | bytes 19660800 | tf_op jit(solution)/shard_map/reduce_scatter | solution.py:27
  84.7 126.9 %copy-start.44 = (bf16[127,80]{0,1:T(8,128)(2,1)S(1)}, bf16[127,80]{0,1:T(8,128)(2,1)}, u32[]{:S(2)}) copy-start(bf16[127,80]{0,1:T(8,128)(2,1)} %param.33) | copy-start | bytes 60964
  84.7 127.2 %copy-start.45 = (bf16[127,80]{0,1:T(8,128)(2,1)S(1)}, bf16[127,80]{0,1:T(8,128)(2,1)}, u32[]{:S(2)}) copy-start(bf16[127,80]{0,1:T(8,128)(2,1)} %param.34) | copy-start | bytes 60964
  84.7 166.8 %all-gather.13.cloned.1.call-start = ((), (), s32[]{:S(2)}) async-start(), calls=%async_computation.11 | async-start | bytes 6553600 | tf_op jit(solution)/shard_map/all_gather | solution.py:36
  211.0 377.3 %all-gather.15.cloned.1.call-start = ((), (), s32[]{:S(2)}) async-start(), calls=%async_computation.12 | async-start | bytes 3276800 | tf_op jit(solution)/shard_map/all_gather | solution.py:23
  268.2 320.1 %copy-start.13 = (bf16[320,320]{1,0:T(8,128)(2,1)S(1)}, bf16[320,320]{1,0:T(8,128)(2,1)}, u32[]{:S(2)}) copy-start(bf16[320,320]{1,0:T(8,128)(2,1)} %param.23) | copy-start | bytes 614404
  562.6 125.3 %reduce-scatter.12.cloned.1.call-start = ((), (), s32[]{:S(2)}) async-start(), calls=%async_computation.13 | async-start | bytes 6553600 | tf_op jit(solution)/shard_map/reduce_scatter | solution.py:31
  593.9 93.9 %copy-start.5 = (bf16[1,1024,320]{1,2,0:T(8,128)(2,1)S(1)}, bf16[1,1024,320]{1,2,0:T(8,128)(2,1)}, u32[]{:S(2)}) copy-start(bf16[1,1024,320]{1,2,0:T(8,128)(2,1)} %param.20) | copy-start | bytes 1966084
  593.9 94.0 %copy-start.40 = (f32[320]{0:T(512)S(1)}, f32[320]{0:T(512)}, u32[]{:S(2)}) copy-start(f32[320]{0:T(512)} %param.24) | copy-start | bytes 3844
  593.9 103.7 %copy-start.31 = (f32[320]{0:T(512)S(1)}, f32[320]{0:T(512)}, u32[]{:S(2)}) copy-start(f32[320]{0:T(512)} %param.27) | copy-start | bytes 3844
  593.9 103.7 %copy-start.41 = (f32[320]{0:T(512)S(1)}, f32[320]{0:T(512)}, u32[]{:S(2)}) copy-start(f32[320]{0:T(512)} %param.28) | copy-start | bytes 3844
  593.9 148.9 %all-gather.27.cloned.1.call-start = ((), (), s32[]{:S(2)}) async-start(), calls=%async_computation.26 | async-start | bytes 3276800 | tf_op jit(solution)/shard_map/all_gather | solution.py:19
  594.5 204.0 %all-gather.17.cloned.1.call-start = ((), (), s32[]{:S(2)}) async-start(), calls=%async_computation.14 | async-start | bytes 3276800 | tf_op jit(solution)/shard_map/all_gather | solution.py:19
  697.5 615.4 %copy-start.19 = (f32[1024]{0:T(1024)}, f32[1024]{0:T(1024)S(1)}, u32[]{:S(2)}) copy-start(f32[1024]{0:T(1024)S(1)} %get-tuple-element.230) | copy-start | bytes 12292
  697.5 615.4 %copy-start.21 = (f32[1024]{0:T(1024)}, f32[1024]{0:T(1024)S(1)}, u32[]{:S(2)}) copy-start(f32[1024]{0:T(1024)S(1)} %get-tuple-element.231) | copy-start | bytes 12292
  700.0 254.9 %reduce-scatter.18.cloned.1.call-start = ((), (), s32[]{:S(2)}) async-start(), calls=%async_computation.18 | async-start | bytes 26214400 | tf_op jit(solution)/shard_map/reduce_scatter | solution.py:27
  754.5 356.3 %reduce-scatter.14.cloned.1.call-start = ((), (), s32[]{:S(2)}) async-start(), calls=%async_computation.15 | async-start | bytes 26214400 | tf_op jit(solution)/shard_map/reduce_scatter | solution.py:27
  812.7 298.1 %copy-start.33 = (f32[1280]{0:T(1024)S(1)}, f32[1280]{0:T(1024)}, u32[]{:S(2)}) copy-start(f32[1280]{0:T(1024)} %param.30) | copy-start | bytes 15364
  812.7 383.8 %all-gather.21.cloned.1.call-start = ((), (), s32[]{:S(2)}) async-start(), calls=%async_computation.19 | async-start | bytes 13107200 | tf_op jit(solution)/shard_map/all_gather | solution.py:23
  1126.1 176.9 %reduce-scatter.20.cloned.1.call-start = ((), (), s32[]{:S(2)}) async-start(), calls=%async_computation.20 | async-start | bytes 6553600 | tf_op jit(solution)/shard_map/reduce_scatter | solution.py:31
  1209.1 103.8 %copy-start.10 = (bf16[1,1024,320]{1,2,0:T(8,128)(2,1)S(1)}, bf16[1,1024,320]{1,2,0:T(8,128)(2,1)}, u32[]{:S(2)}) copy-start(bf16[1,1024,320]{1,2,0:T(8,128)(2,1)} %param.35) | copy-start | bytes 1966084
  1209.1 159.5 %all-gather.23.cloned.1.call-start = ((), (), s32[]{:S(2)}) async-start(), calls=%async_computation.21 | async-start | bytes 3276800 | tf_op jit(solution)/shard_map/all_gather | solution.py:19
  1315.9 110.5 %reduce-scatter.22.cloned.1.call-start = ((), (), s32[]{:S(2)}) async-start(), calls=%async_computation.22 | async-start | bytes 6553600 | tf_op jit(solution)/shard_map/reduce_scatter | solution.py:27
  1374.3 724.1 %reduce-scatter.24.cloned.1.call-start = ((), (), s32[]{:S(2)}) async-start(), calls=%async_computation.23 | async-start | bytes 13107200 | tf_op jit(solution)/shard_map/reduce_scatter | solution.py:27
  2012.9 157.2 %all-gather.19.cloned.1.call-start = ((), (), s32[]{:S(2)}) async-start(), calls=%async_computation.16 | async-start | bytes 13107200 | tf_op jit(solution)/shard_map/all_gather | solution.py:23
  2019.9 80.4 %copy-start.18 = (bf16[4,1024,80]{1,2,0:T(8,128)(2,1)S(1)}, bf16[4,1024,80]{1,2,0:T(8,128)(2,1)}, u32[]{:S(2)}) copy-start(bf16[4,1024,80]{1,2,0:T(8,128)(2,1)} %get-tuple-element.132) | copy-start | bytes 1966084
  2019.9 207.0 %all-gather.25.cloned.1.call-start = ((), (), s32[]{:S(2)}) async-start(), calls=%async_computation.24 | async-start | bytes 9830400 | tf_op jit(solution)/shard_map/all_gather | solution.py:23
  2101.8 208.8 %all-reduce.13.cloned.1.call-start = ((), (), s32[]{:S(2)}) async-start(), calls=%async_computation.28 | async-start | bytes 5242880 | tf_op jit(solution)/shard_map/psum | solution.py:283
  2235.4 171.2 %reduce-scatter.26.cloned.1.call-start = ((), (), s32[]{:S(2)}) async-start(), calls=%async_computation.25 | async-start | bytes 6553600 | tf_op jit(solution)/shard_map/reduce_scatter | solution.py:31
  2243.4 259.8 %reduce-scatter.16.cloned.1.call-start = ((), (), s32[]{:S(2)}) async-start(), calls=%async_computation.17 | async-start | bytes 6553600 | tf_op jit(solution)/shard_map/reduce_scatter | solution.py:31
  2257.3 375.4 %all-reduce.11.cloned.1.call-start = ((), (), s32[]{:S(2)}) async-start(), calls=%async_computation.27 | async-start | bytes 163840 | tf_op jit(solution)/shard_map/psum | solution.py:272
  2277.9 128.8 %copy-start.6 = (bf16[1,1024,320]{1,2,0:T(8,128)(2,1)S(1)}, bf16[1,1024,320]{1,2,0:T(8,128)(2,1)}, u32[]{:S(2)}) copy-start(bf16[1,1024,320]{1,2,0:T(8,128)(2,1)} %param.20) | copy-start | bytes 1966084
  2277.9 128.8 %copy-start.24 = (f32[1024]{0:T(1024)S(1)}, f32[1024]{0:T(1024)}, u32[]{:S(2)}) copy-start(f32[1024]{0:T(1024)} %copy-done.23) | copy-start | bytes 12292
  2277.9 128.8 %copy-start.26 = (f32[1024]{0:T(1024)S(1)}, f32[1024]{0:T(1024)}, u32[]{:S(2)}) copy-start(f32[1024]{0:T(1024)} %copy-done.25) | copy-start | bytes 12292
  2277.9 128.7 %copy-start.35 = (f32[320]{0:T(512)S(1)}, f32[320]{0:T(512)}, u32[]{:S(2)}) copy-start(f32[320]{0:T(512)} %param.25) | copy-start | bytes 3844
  2277.9 225.3 %copy-start.4 = (f32[1024,320]{0,1:T(8,128)S(1)}, f32[1024,320]{0,1:T(8,128)}, u32[]{:S(2)}) copy-start(f32[1024,320]{0,1:T(8,128)} %get-tuple-element.219) | copy-start | bytes 3932164
  2277.9 225.3 %copy-start.11 = (bf16[1,1024,320]{1,2,0:T(8,128)(2,1)S(1)}, bf16[1,1024,320]{1,2,0:T(8,128)(2,1)}, u32[]{:S(2)}) copy-start(bf16[1,1024,320]{1,2,0:T(8,128)(2,1)} %param.35) | copy-start | bytes 1966084
  2277.9 225.3 %copy-start.20 = (f32[1024]{0:T(1024)S(1)}, f32[1024]{0:T(1024)}, u32[]{:S(2)}) copy-start(f32[1024]{0:T(1024)} %copy-done.19) | copy-start | bytes 12292
  2277.9 225.3 %copy-start.22 = (f32[1024]{0:T(1024)S(1)}, f32[1024]{0:T(1024)}, u32[]{:S(2)}) copy-start(f32[1024]{0:T(1024)} %copy-done.21) | copy-start | bytes 12292
  2277.9 225.3 %copy-start.28 = (f32[1024]{0:T(1024)S(1)}, f32[1024]{0:T(1024)}, u32[]{:S(2)}) copy-start(f32[1024]{0:T(1024)} %copy-done.27) | copy-start | bytes 12292
  2277.9 225.3 %copy-start.30 = (f32[1024]{0:T(1024)S(1)}, f32[1024]{0:T(1024)}, u32[]{:S(2)}) copy-start(f32[1024]{0:T(1024)} %copy-done.29) | copy-start | bytes 12292
  2278.0 225.3 %copy-start.32 = (f32[320]{0:T(512)S(1)}, f32[320]{0:T(512)}, u32[]{:S(2)}) copy-start(f32[320]{0:T(512)} %param.27) | copy-start | bytes 3844
  2278.0 225.3 %copy-start.39 = (f32[320]{0:T(512)S(1)}, f32[320]{0:T(512)}, u32[]{:S(2)}) copy-start(f32[320]{0:T(512)} %param.32) | copy-start | bytes 3844
  2317.2 318.4 %copy-start.1 = (bf16[320,1280]{1,0:T(8,128)(2,1)S(1)}, bf16[320,1280]{1,0:T(8,128)(2,1)}, u32[]{:S(2)}) copy-start(bf16[320,1280]{1,0:T(8,128)(2,1)} %param.29) | copy-start | bytes 2457604
  2318.5 189.1 %copy-start.36 = (f32[320]{0:T(512)S(1)}, f32[320]{0:T(512)}, u32[]{:S(2)}) copy-start(f32[320]{0:T(512)} %get-tuple-element.141) | copy-start | bytes 3844
  2318.5 189.1 %copy-start.37 = (f32[320]{0:T(512)S(1)}, f32[320]{0:T(512)}, u32[]{:S(2)}) copy-start(f32[320]{0:T(512)} %get-tuple-element.147) | copy-start | bytes 3844
  (24 other events, 407.2 us)
Sparse Core Ops, SparseCore 0:
  19.8 53.1 all-gather.10
  84.8 120.4 reduce-scatter.9
  211.1 40.4 all-gather.12
  562.7 25.5 all-gather.14
  594.0 93.7 reduce-scatter.11
  689.2 53.4 all-gather.26
  744.9 53.5 all-gather.16
  801.1 153.7 reduce-scatter.17
  957.7 153.1 reduce-scatter.13
  1126.3 70.1 all-gather.20
  1209.3 93.7 reduce-scatter.19
  1316.1 52.5 all-gather.22
  1374.4 51.9 reduce-scatter.21
  2013.0 85.3 reduce-scatter.23
  2099.8 70.1 all-gather.18
  2171.6 55.3 all-gather.24
  2235.5 75.0 all-reduce.12
  2312.8 93.8 reduce-scatter.25
  2408.9 94.2 reduce-scatter.15
  2509.3 123.4 all-reduce.10
where the time goes:
time: 2660 us; the launch traced here: 2640 us
  waiting for transfers between devices  1470 us (55%)
  matrix products  398 us (15%)
  local copies, waits for them, and re-layouts  380 us (14%)
  other arithmetic  324 us (12%)
  blocking collectives  52.3 us (2%)
    reduce_scatter x5, waiting for transfers between devices, sum_over_row(): return lax.psum_scatter(values, 'row', scatter_dimension=0, tiled=True)  548 us
    reduce_scatter x4, waiting for transfers between devices, sum_over_col(): return lax.psum_scatter(values, 'col', scatter_dimension=0, tiled=True)  363 us
    add x8, local copies, waits for them, and re-layouts, head_scores(): rel_rows[:, :, :, None] + rel_cols[:, :, None, :]  223 us
    all_gather x4, waiting for transfers between devices, rows_over_row(): return lax.all_gather(values, 'row', axis=0, tiled=True)  202 us
    all_gather x4, waiting for transfers between devices, rows_over_col(): return lax.all_gather(values, 'col', axis=0, tiled=True)  193 us
    dot_general x8, matrix products, head_scores(): jnp.einsum('qc,kc->qk', query_one, key_one, preferred_element_type=jnp.fl...  124 us
    psum x1, waiting for transfers between devices, shards(): lax.psum((height_part, width_part), ('batch', 'row', 'col'))  106 us
    reshape x4, local copies, waits for them, and re-layouts, attend_back(): score_grad.astype(jnp.float32)  96.1 us
  transfers between devices with their start and end apart: 20, of which 20 were waited for; matrix products, arithmetic and copies ran while one was open for 5% of the time, Pallas kernels for 0%

commit v1 on v0

--- a/solution.py
+++ b/solution.py
@@ -11,12 +11,25 @@
 HIGHEST = lax.Precision.HIGHEST
 
 
+def ring_gather(value, axis, dim):
+    ways = lax.axis_size(axis)
+    up = [(d, (d + 1) % ways) for d in range(ways)]
+    down = [(d, (d - 1) % ways) for d in range(ways)]
+    earlier, later = ([value], [value])
+    for _ in range(ways // 2):
+        earlier.append(lax.ppermute(earlier[-1], axis, up))
+    for _ in range((ways - 1) // 2):
+        later.append(lax.ppermute(later[-1], axis, down))
+    line = jnp.concatenate([*earlier[::-1], *later[1:]], axis=dim)
+    return jnp.roll(line, (lax.axis_index(axis) - ways // 2) * value.shape[dim], axis=dim)
+
+
 def feature_sums(first, second):
     return lax.psum((first, second), "row")
 
 
 def rows_over_col(values):
-    return lax.all_gather(values, "col", axis=0, tiled=True)
+    return ring_gather(values, "col", 0)
 
 
 def rows_over_row(values):

time: 2660 us -> 2570 us (0.966)
  waiting for transfers between devices: 1470 us -> 1350 us
    ppermute x0 -> x12, waiting for transfers between devices: none -> 200 us  [the longest x8 169 us: ring_gather(): earlier.append(lax.ppermute(earlier[-1], axis, up))]
    all_gather x4 -> x0, waiting for transfers between devices: 193 us -> none  [rows_over_col(): return lax.all_gather(values, 'col', axis=0, tiled=True)]
    reduce_scatter x4, waiting for transfers between devices: 363 us -> 287 us  [sum_over_col(): return lax.psum_scatter(values, 'col', scatter_dimension=0, tiled=True)]
    reduce_scatter x5, waiting for transfers between devices: 548 us -> 491 us  [sum_over_row(): return lax.psum_scatter(values, 'row', scatter_dimension=0, tiled=True)]
  transfers between devices with their start and end apart: 20 -> 28, of which waited for: 20 -> 28; matrix products, arithmetic and copies ran while one was open for 5% -> 5% of each run, Pallas kernels for 0% -> 0%
where the time goes in v1:
time: 2570 us; the launch traced here: 2560 us
  waiting for transfers between devices  1350 us (53%)
  local copies, waits for them, and re-layouts  386 us (15%)
  matrix products  385 us (15%)
  other arithmetic  347 us (14%)
  blocking collectives  51.1 us (2%)
  starting transfers between devices  26.7 us (1%)
    reduce_scatter x5, waiting for transfers between devices, sum_over_row(): return lax.psum_scatter(values, 'row', scatter_dimension=0, tiled=True)  491 us
    reduce_scatter x4, waiting for transfers between devices, sum_over_col(): return lax.psum_scatter(values, 'col', scatter_dimension=0, tiled=True)  287 us
    add x8, local copies, waits for them, and re-layouts, head_scores(): rel_rows[:, :, :, None] + rel_cols[:, :, None, :]  223 us
    all_gather x4, waiting for transfers between devices, rows_over_row(): return lax.all_gather(values, 'row', axis=0, tiled=True)  202 us
    ppermute x8, waiting for transfers between devices, ring_gather(): earlier.append(lax.ppermute(earlier[-1], axis, up))  169 us
    dot_general x8, matrix products, head_scores(): jnp.einsum('qc,kc->qk', query_one, key_one, preferred_element_type=jnp.fl...  124 us
    psum x1, waiting for transfers between devices, shards(): lax.psum((height_part, width_part), ('batch', 'row', 'col'))  106 us
    reshape x4, local copies, waits for them, and re-layouts, attend_back(): score_grad.astype(jnp.float32)  95.9 us
  transfers between devices with their start and end apart: 28, of which 28 were waited for; matrix products, arithmetic and copies ran while one was open for 5% of the time, Pallas kernels for 0%

profile of v1, /device:TPU:8, one launch (start us, length us, event | category | flops | bytes accessed | tf_op | source)
XLA Modules:
  0.0 2556.5 jit_solution(11635811184847515371)
XLA Ops:
  20.3 25.5 collective-permute-done
  76.8 120.5 %reduce-scatter.10.cloned.1.call-done = f32[1024,3,320]{0,2,1:T(8,128)} async-done(((f32[4096,3,320]{0,2,1:T(8,128)}), f32[1024,3,320]{0,2,1:T(8,128)}) %reduce-scatter.10.cloned.1.call-update) | async-done | bytes 3932176 | tf_op jit(solution)/shard_map/reduce_scatter | solution.py:40
  209.9 33.7 %all-gather.6.cloned.1.call-done = bf16[4096,2,320]{0,2,1:T(8,128)(2,1)} async-done(((bf16[1024,2,320]{0,2,1:T(8,128)(2,1)}), bf16[4096,2,320]{0,2,1:T(8,128)(2,1)}) %all-gather.6.cloned.1.call-update) | async-done | bytes 5242896 | tf_op jit(solution)/shard_map/all_gather | solution.py:49
  260.2 293.7 %while.30 = (s32[]{:T(128)}, bf16[4,1024,80]{1,2,0:T(8,128)(2,1)S(1)}, f32[4,1024]{1,0:T(4,128)}, bf16[4,1024,80]{2,1,0:T(8,128)(2,1)}, bf16[4,4096,80]{2,1,0:T(...) while((s32[]{:T(128)}, ...), condition=%wide.region_8.10_spmd, body=%wide.region_5.9_spmd.sunk | while | flops 1400978432 | bytes 123054200 | solution.py:163
  273.7 27.9 %add.352 = f32[1024,4096]{1,0:T(8,128)} reshape(f32[16,64,64,64]{3,2,1,0:T(8,128)} %broadcast_add_fusion.4) | data formatting | bytes 33554432 | tf_op jit(solution)/shard_map/while/body/eval_jaxpr/add | solution.py:86
  301.6 14.6 fusion.222
  347.1 27.9 %add.352 = f32[1024,4096]{1,0:T(8,128)} reshape(f32[16,64,64,64]{3,2,1,0:T(8,128)} %broadcast_add_fusion.4) | data formatting | bytes 33554432 | tf_op jit(solution)/shard_map/while/body/eval_jaxpr/add | solution.py:86
  375.1 14.6 fusion.222
  420.5 27.9 %add.352 = f32[1024,4096]{1,0:T(8,128)} reshape(f32[16,64,64,64]{3,2,1,0:T(8,128)} %broadcast_add_fusion.4) | data formatting | bytes 33554432 | tf_op jit(solution)/shard_map/while/body/eval_jaxpr/add | solution.py:86
  448.5 14.6 fusion.222
  494.0 27.9 %add.352 = f32[1024,4096]{1,0:T(8,128)} reshape(f32[16,64,64,64]{3,2,1,0:T(8,128)} %broadcast_add_fusion.4) | data formatting | bytes 33554432 | tf_op jit(solution)/shard_map/while/body/eval_jaxpr/add | solution.py:86
  555.2 25.2 all-gather.8.cloned.1.call-done
  588.3 38.0 %collective-permute-done.6 = bf16[1024,320]{0,1:T(8,128)(2,1)S(1)} collective-permute-done((bf16[1024,320]{0,1:T(8,128)(2,1)S(1)}, bf16[1024,320]{0,1:T(8,128)(2,1)S(1)}, u32[]{:S(2)}, u32[]{:S(2)}) %collective-permute-start.6) | collective-permute-done | bytes 655392 | tf_op jit(solution)/shard_map/ppermute | solution.py:20
  651.4 28.7 %collective-permute-done.7 = bf16[1024,320]{0,1:T(8,128)(2,1)S(1)} collective-permute-done((bf16[1024,320]{0,1:T(8,128)(2,1)S(1)}, bf16[1024,320]{0,1:T(8,128)(2,1)S(1)}, u32[]{:S(2)}, u32[]{:S(2)}) %collective-permute-start.7) | collective-permute-done | bytes 655392 | tf_op jit(solution)/shard_map/ppermute | solution.py:20
  700.1 17.8 reduce-scatter.12.cloned.1.call-done
  730.2 15.6 collective-permute-done.3
  788.7 84.1 %reduce-scatter.18.cloned.1.call-done = f32[1024,1280]{1,0:T(8,128)} async-done(((f32[4096,1280]{1,0:T(8,128)}), f32[1024,1280]{1,0:T(8,128)}) %reduce-scatter.18.cloned.1.call-update) | async-done | bytes 5242896 | tf_op jit(solution)/shard_map/reduce_scatter | solution.py:40
  872.8 155.8 %reduce-scatter.14.cloned.1.call-done = f32[1024,1280]{1,0:T(8,128)} async-done(((f32[4096,1280]{1,0:T(8,128)}), f32[1024,1280]{1,0:T(8,128)}) %reduce-scatter.14.cloned.1.call-update) | async-done | bytes 5242896 | tf_op jit(solution)/shard_map/reduce_scatter | solution.py:40
  1028.6 15.2 add_convert_fusion
  1043.9 70.3 %all-gather.12.cloned.1.call-done = bf16[4096,1280]{1,0:T(8,128)(2,1)} async-done(((bf16[1024,1280]{1,0:T(8,128)(2,1)}), bf16[4096,1280]{1,0:T(8,128)(2,1)}) %all-gather.12.cloned.1.call-update) | async-done | bytes 10485776 | tf_op jit(solution)/shard_map/all_gather | solution.py:36
  1126.8 93.9 %reduce-scatter.20.cloned.1.call-done = f32[1024,320]{0,1:T(8,128)} async-done(((f32[4096,320]{0,1:T(8,128)}), f32[1024,320]{0,1:T(8,128)}) %reduce-scatter.20.cloned.1.call-update) | async-done | bytes 1310736 | tf_op jit(solution)/shard_map/reduce_scatter | solution.py:44
  1234.8 26.4 %collective-permute-done.9 = bf16[1024,320]{0,1:T(8,128)(2,1)S(1)} collective-permute-done((bf16[1024,320]{0,1:T(8,128)(2,1)S(1)}, bf16[1024,320]{0,1:T(8,128)(2,1)S(1)}, u32[]{:S(2)}, u32[]{:S(2)}) %collective-permute-start.9) | collective-permute-done | bytes 655392 | tf_op jit(solution)/shard_map/ppermute | solution.py:20
  1290.2 52.2 %reduce-scatter.22.cloned.1.call-done = f32[1024,320]{0,1:T(8,128)} async-done(((f32[4096,320]{0,1:T(8,128)}), f32[1024,320]{0,1:T(8,128)}) %reduce-scatter.22.cloned.1.call-update) | async-done | bytes 1310736 | tf_op jit(solution)/shard_map/reduce_scatter | solution.py:40
  1345.1 574.5 %while.31 = (s32[]{:T(128)}, bf16[4,1024,80]{1,2,0:T(8,128)(2,1)}, f32[4,4096,80]{1,2,0:T(8,128)}, f32[4,4096,80]{1,2,0:T(8,128)}, f32[4,16,64,80]{3,2,1,0:T(8,1...) while((s32[]{:T(128)}, bf16[4,1024,80]{1,2,0:T(8,128)(2,1)}, ...), condition=%wide.region_27.29_spmd, body=%wide.region_23.28_spmd.sunk | while | flops 3678845952 | bytes 353068224 | solution.py:249
  1369.0 27.9 %add.359 = f32[1024,4096]{1,0:T(8,128)} reshape(f32[16,64,64,64]{3,2,1,0:T(8,128)} %broadcast_add_fusion.5) | data formatting | bytes 33554432 | tf_op jit(solution)/shard_map/while/body/eval_jaxpr/add | solution.py:86
  1396.9 16.5 multiply_reduce_fusion.7
  1436.3 24.0 reshape.155
  1460.2 15.4 fusion.247
  1512.5 27.9 %add.359 = f32[1024,4096]{1,0:T(8,128)} reshape(f32[16,64,64,64]{3,2,1,0:T(8,128)} %broadcast_add_fusion.5) | data formatting | bytes 33554432 | tf_op jit(solution)/shard_map/while/body/eval_jaxpr/add | solution.py:86
  1540.4 16.5 multiply_reduce_fusion.7
  1579.7 24.0 reshape.155
  1603.7 15.4 fusion.247
  1656.0 27.9 %add.359 = f32[1024,4096]{1,0:T(8,128)} reshape(f32[16,64,64,64]{3,2,1,0:T(8,128)} %broadcast_add_fusion.5) | data formatting | bytes 33554432 | tf_op jit(solution)/shard_map/while/body/eval_jaxpr/add | solution.py:86
  1683.9 16.5 multiply_reduce_fusion.7
  1723.2 24.0 reshape.155
  1747.2 15.4 fusion.247
  1799.4 27.9 %add.359 = f32[1024,4096]{1,0:T(8,128)} reshape(f32[16,64,64,64]{3,2,1,0:T(8,128)} %broadcast_add_fusion.5) | data formatting | bytes 33554432 | tf_op jit(solution)/shard_map/while/body/eval_jaxpr/add | solution.py:86
  1827.3 16.5 multiply_reduce_fusion.7
  1866.7 24.0 reshape.155
  1890.6 15.4 fusion.247
  1935.8 78.4 %reduce-scatter.24.cloned.1.call-done = f32[1024,2,320]{0,2,1:T(8,128)} async-done(((f32[4096,2,320]{0,2,1:T(8,128)}), f32[1024,2,320]{0,2,1:T(8,128)}) %reduce-scatter.24.cloned.1.call-update) | async-done | bytes 2621456 | tf_op jit(solution)/shard_map/reduce_scatter | solution.py:40
  2027.3 58.7 %all-gather.10.cloned.1.call-done = bf16[4096,1280]{1,0:T(8,128)(2,1)} async-done(((bf16[1024,1280]{1,0:T(8,128)(2,1)}), bf16[4096,1280]{1,0:T(8,128)(2,1)}) %all-gather.10.cloned.1.call-update) | async-done | bytes 10485776 | tf_op jit(solution)/shard_map/all_gather | solution.py:36
  2095.6 47.3 %all-gather.14.cloned.1.call-done = bf16[4096,3,320]{0,2,1:T(8,128)(2,1)} async-done(((bf16[1024,3,320]{0,2,1:T(8,128)(2,1)}), bf16[4096,3,320]{0,2,1:T(8,128)(2,1)}) %all-gather.14.cloned.1.call-update) | async-done | bytes 7864336 | tf_op jit(solution)/shard_map/all_gather | solution.py:36
  2198.8 26.1 %all-reduce.13.cloned.1.call-done = (bf16[320,3,320]{2,0,1:T(8,128)(2,1)}, bf16[320,320]{1,0:T(8,128)(2,1)}, bf16[320,1280]{1,0:T(8,128)(2,1)}, bf16[1280,320]{0,1:T(8,128)(2,1)}) async-done(((bf16[320,3,320]{2,0,1:T(8,128)(2,1)}, bf16[320,320]{1,0:T(8,128)(2,1)}, bf16[320,1280]{1,0:T(8,128)(2,1)}, bf16[1280,320]{0,1:T(8,128)(2,1)}), (bf16[320,3,320]{2,0,1:T(8,128)(2,1)}, bf16[320,320]{1,0:T(8,128)(2,1)}, ...) | async-done | bytes 2457616 | tf_op jit(solution)/shard_map/psum | solution.py:296
  2232.7 88.1 %reduce-scatter.26.cloned.1.call-done = f32[1024,320]{0,1:T(8,128)} async-done(((f32[4096,320]{0,1:T(8,128)}), f32[1024,320]{0,1:T(8,128)}) %reduce-scatter.26.cloned.1.call-update) | async-done | bytes 1310736 | tf_op jit(solution)/shard_map/reduce_scatter | solution.py:44
  2329.8 87.5 %reduce-scatter.16.cloned.1.call-done = f32[1024,320]{0,1:T(8,128)} async-done(((f32[4096,320]{0,1:T(8,128)}), f32[1024,320]{0,1:T(8,128)}) %reduce-scatter.16.cloned.1.call-update) | async-done | bytes 1310736 | tf_op jit(solution)/shard_map/reduce_scatter | solution.py:44
  2421.7 19.1 all-reduce.1
  2440.8 106.1 %all-reduce.11.cloned.1.call-done = (f32[127,80]{0,1:T(8,128)}, f32[127,80]{0,1:T(8,128)}) async-done(((f32[127,80]{0,1:T(8,128)}, f32[127,80]{0,1:T(8,128)}), (f32[127,80]{0,1:T(8,128)}, f32[127,80]{0,1:T(8,128)})) %all-reduce.11.cloned.1.call-update) | async-done | bytes 81296 | tf_op jit(solution)/shard_map/psum | solution.py:285
  (354 shorter events, 736.1 us)
Async XLA Ops:
  7.2 771.4 %copy-start = (bf16[320,1280]{1,0:T(8,128)(2,1)S(1)}, bf16[320,1280]{1,0:T(8,128)(2,1)}, u32[]{:S(2)}) copy-start(bf16[320,1280]{1,0:T(8,128)(2,1)} %param.31) | copy-start | bytes 2457604
  7.2 190.1 %reduce-scatter.10.cloned.1.call-start = ((), (), s32[]{:S(2)}) async-start(), calls=%async_computation.9 | async-start | bytes 19660800 | tf_op jit(solution)/shard_map/reduce_scatter | solution.py:40
  18.3 27.6 %collective-permute-start = (bf16[1024,320]{0,1:T(8,128)(2,1)S(1)}, bf16[1024,320]{0,1:T(8,128)(2,1)S(1)}, u32[]{:S(2)}, u32[]{:S(2)}) collective-permute-start(bf16[1024,320]{0,1:T(8,128)(2,1)S(1)} %fusion.96), channel_id=1, source_target_pairs={{0,1},{1,2},{2,3},{3,0},{4,5},{5,6},{6,7},{7,4},{8,9},{9,10},{10,1... | collective-permute-start | bytes 1966088 | tf_op jit(solution)/shard_map/ppermute | solution.py:20
  19.9 30.8 %collective-permute-start.2 = (bf16[1024,320]{0,1:T(8,128)(2,1)S(1)}, bf16[1024,320]{0,1:T(8,128)(2,1)S(1)}, u32[]{:S(2)}, u32[]{:S(2)}) collective-permute-start(bf16[1024,320]{0,1:T(8,128)(2,1)S(1)} %fusion.96), channel_id=1, source_target_pairs={{0,3},{1,0},{2,1},{3,2},{4,7},{5,4},{6,5},{7,6},{8,11},{9,8},{10,9... | collective-permute-start | bytes 1966088 | tf_op jit(solution)/shard_map/ppermute | solution.py:22
  45.9 15.9 collective-permute-start.1
  76.2 167.4 %all-gather.6.cloned.1.call-start = ((), (), s32[]{:S(2)}) async-start(), calls=%async_computation.10 | async-start | bytes 6553600 | tf_op jit(solution)/shard_map/all_gather | solution.py:49
  203.0 377.4 %all-gather.8.cloned.1.call-start = ((), (), s32[]{:S(2)}) async-start(), calls=%async_computation.11 | async-start | bytes 3276800 | tf_op jit(solution)/shard_map/all_gather | solution.py:36
  260.2 320.3 %copy-start.18 = (bf16[320,320]{1,0:T(8,128)(2,1)S(1)}, bf16[320,320]{1,0:T(8,128)(2,1)}, u32[]{:S(2)}) copy-start(bf16[320,320]{1,0:T(8,128)(2,1)} %param.25) | copy-start | bytes 614404
  554.8 163.1 %reduce-scatter.12.cloned.1.call-start = ((), (), s32[]{:S(2)}) async-start(), calls=%async_computation.12 | async-start | bytes 6553600 | tf_op jit(solution)/shard_map/reduce_scatter | solution.py:44
  586.1 286.7 %reduce-scatter.18.cloned.1.call-start = ((), (), s32[]{:S(2)}) async-start(), calls=%async_computation.16 | async-start | bytes 26214400 | tf_op jit(solution)/shard_map/reduce_scatter | solution.py:40
  586.2 40.1 %collective-permute-start.6 = (bf16[1024,320]{0,1:T(8,128)(2,1)S(1)}, bf16[1024,320]{0,1:T(8,128)(2,1)S(1)}, u32[]{:S(2)}, u32[]{:S(2)}) collective-permute-start(bf16[1024,320]{0,1:T(8,128)(2,1)S(1)} %bitcast.279), channel_id=1, source_target_pairs={{0,1},{1,2},{2,3},{3,0},{4,5},{5,6},{6,7},{7,4},{8,9},{9,10},{10,1... | collective-permute-start | bytes 1966088 | tf_op jit(solution)/shard_map/ppermute | solution.py:20
  587.7 63.6 %collective-permute-start.8 = (bf16[1024,320]{0,1:T(8,128)(2,1)S(1)}, bf16[1024,320]{0,1:T(8,128)(2,1)S(1)}, u32[]{:S(2)}, u32[]{:S(2)}) collective-permute-start(bf16[1024,320]{0,1:T(8,128)(2,1)S(1)} %bitcast.280), channel_id=1, source_target_pairs={{0,3},{1,0},{2,1},{3,2},{4,7},{5,4},{6,5},{7,6},{8,11},{9,8},{10,9... | collective-permute-start | bytes 1966088 | tf_op jit(solution)/shard_map/ppermute | solution.py:22
  626.3 53.8 %collective-permute-start.7 = (bf16[1024,320]{0,1:T(8,128)(2,1)S(1)}, bf16[1024,320]{0,1:T(8,128)(2,1)S(1)}, u32[]{:S(2)}, u32[]{:S(2)}) collective-permute-start(bf16[1024,320]{0,1:T(8,128)(2,1)S(1)} %collective-permute-done.6), channel_id=1, source_target_pairs={{0,1},{1,2},{2,3},{3,0},{4,5},{5,6},{6,7},{7,4},{8,9},{9,10},{10,1... | collective-permute-start | bytes 1966088 | tf_op jit(solution)/shard_map/ppermute | solution.py:20
  700.1 328.6 %reduce-scatter.14.cloned.1.call-start = ((), (), s32[]{:S(2)}) async-start(), calls=%async_computation.13 | async-start | bytes 26214400 | tf_op jit(solution)/shard_map/reduce_scatter | solution.py:40
  726.4 504.1 %copy-start.26 = (f32[1024]{0:T(1024)}, f32[1024]{0:T(1024)S(1)}, u32[]{:S(2)}) copy-start(f32[1024]{0:T(1024)S(1)} %get-tuple-element.235) | copy-start | bytes 12292
  726.5 504.1 %copy-start.28 = (f32[1024]{0:T(1024)}, f32[1024]{0:T(1024)S(1)}, u32[]{:S(2)}) copy-start(f32[1024]{0:T(1024)S(1)} %get-tuple-element.236) | copy-start | bytes 12292
  728.1 17.7 collective-permute-start.3
  729.0 31.2 %collective-permute-start.5 = (bf16[1024,320]{0,1:T(8,128)(2,1)S(1)}, bf16[1024,320]{0,1:T(8,128)(2,1)S(1)}, u32[]{:S(2)}, u32[]{:S(2)}) collective-permute-start(bf16[1024,320]{0,1:T(8,128)(2,1)S(1)} %add_convert_fusion.3), channel_id=1, source_target_pairs={{0,3},{1,0},{2,1},{3,2},{4,7},{5,4},{6,5},{7,6},{8,11},{9,8},{10,9... | collective-permute-start | bytes 1966088 | tf_op jit(solution)/shard_map/ppermute | solution.py:22
  745.8 26.8 %collective-permute-start.4 = (bf16[1024,320]{0,1:T(8,128)(2,1)S(1)}, bf16[1024,320]{0,1:T(8,128)(2,1)S(1)}, u32[]{:S(2)}, u32[]{:S(2)}) collective-permute-start(bf16[1024,320]{0,1:T(8,128)(2,1)S(1)} %collective-permute-done.3), channel_id=1, source_target_pairs={{0,1},{1,2},{2,3},{3,0},{4,5},{5,6},{6,7},{7,4},{8,9},{9,10},{10,1... | collective-permute-start | bytes 1966088 | tf_op jit(solution)/shard_map/ppermute | solution.py:20
  788.6 240.0 %copy-start.40 = (f32[1280]{0:T(1024)S(1)}, f32[1280]{0:T(1024)}, u32[]{:S(2)}) copy-start(f32[1280]{0:T(1024)} %param.32) | copy-start | bytes 15364
  788.6 325.6 %all-gather.12.cloned.1.call-start = ((), (), s32[]{:S(2)}) async-start(), calls=%async_computation.17 | async-start | bytes 13107200 | tf_op jit(solution)/shard_map/all_gather | solution.py:36
  1043.9 176.8 %reduce-scatter.20.cloned.1.call-start = ((), (), s32[]{:S(2)}) async-start(), calls=%async_computation.18 | async-start | bytes 6553600 | tf_op jit(solution)/shard_map/reduce_scatter | solution.py:44
  1126.8 215.6 %reduce-scatter.22.cloned.1.call-start = ((), (), s32[]{:S(2)}) async-start(), calls=%async_computation.19 | async-start | bytes 6553600 | tf_op jit(solution)/shard_map/reduce_scatter | solution.py:40
  1232.7 28.5 %collective-permute-start.9 = (bf16[1024,320]{0,1:T(8,128)(2,1)S(1)}, bf16[1024,320]{0,1:T(8,128)(2,1)S(1)}, u32[]{:S(2)}, u32[]{:S(2)}) collective-permute-start(bf16[1024,320]{0,1:T(8,128)(2,1)S(1)} %fusion.120), channel_id=1, source_target_pairs={{0,1},{1,2},{2,3},{3,0},{4,5},{5,6},{6,7},{7,4},{8,9},{9,10},{10,1... | collective-permute-start | bytes 1966088 | tf_op jit(solution)/shard_map/ppermute | solution.py:20
  1234.8 30.5 %collective-permute-start.11 = (bf16[1024,320]{0,1:T(8,128)(2,1)S(1)}, bf16[1024,320]{0,1:T(8,128)(2,1)S(1)}, u32[]{:S(2)}, u32[]{:S(2)}) collective-permute-start(bf16[1024,320]{0,1:T(8,128)(2,1)S(1)} %fusion.120), channel_id=1, source_target_pairs={{0,3},{1,0},{2,1},{3,2},{4,7},{5,4},{6,5},{7,6},{8,11},{9,8},{10,9... | collective-permute-start | bytes 1966088 | tf_op jit(solution)/shard_map/ppermute | solution.py:22
  1261.3 14.9 collective-permute-start.10
  1290.1 724.1 %reduce-scatter.24.cloned.1.call-start = ((), (), s32[]{:S(2)}) async-start(), calls=%async_computation.20 | async-start | bytes 13107200 | tf_op jit(solution)/shard_map/reduce_scatter | solution.py:40
  1928.7 157.3 %all-gather.10.cloned.1.call-start = ((), (), s32[]{:S(2)}) async-start(), calls=%async_computation.14 | async-start | bytes 13107200 | tf_op jit(solution)/shard_map/all_gather | solution.py:36
  1935.8 207.2 %all-gather.14.cloned.1.call-start = ((), (), s32[]{:S(2)}) async-start(), calls=%async_computation.21 | async-start | bytes 9830400 | tf_op jit(solution)/shard_map/all_gather | solution.py:36
  2017.7 207.2 %all-reduce.13.cloned.1.call-start = ((), (), s32[]{:S(2)}) async-start(), calls=%async_computation.24 | async-start | bytes 5242880 | tf_op jit(solution)/shard_map/psum | solution.py:296
  2149.8 171.1 %reduce-scatter.26.cloned.1.call-start = ((), (), s32[]{:S(2)}) async-start(), calls=%async_computation.22 | async-start | bytes 6553600 | tf_op jit(solution)/shard_map/reduce_scatter | solution.py:44
  2157.8 259.6 %reduce-scatter.16.cloned.1.call-start = ((), (), s32[]{:S(2)}) async-start(), calls=%async_computation.15 | async-start | bytes 6553600 | tf_op jit(solution)/shard_map/reduce_scatter | solution.py:44
  2171.7 375.2 %all-reduce.11.cloned.1.call-start = ((), (), s32[]{:S(2)}) async-start(), calls=%async_computation.23 | async-start | bytes 163840 | tf_op jit(solution)/shard_map/psum | solution.py:285
  2191.1 129.8 %copy-start.6 = (bf16[1,1024,320]{1,2,0:T(8,128)(2,1)S(1)}, bf16[1,1024,320]{1,2,0:T(8,128)(2,1)}, u32[]{:S(2)}) copy-start(bf16[1,1024,320]{1,2,0:T(8,128)(2,1)} %param.22) | copy-start | bytes 1966084
  2191.2 129.7 %copy-start.31 = (f32[1024]{0:T(1024)S(1)}, f32[1024]{0:T(1024)}, u32[]{:S(2)}) copy-start(f32[1024]{0:T(1024)} %copy-done.30) | copy-start | bytes 12292
  2191.2 129.7 %copy-start.33 = (f32[1024]{0:T(1024)S(1)}, f32[1024]{0:T(1024)}, u32[]{:S(2)}) copy-start(f32[1024]{0:T(1024)} %copy-done.32) | copy-start | bytes 12292
  2191.2 129.7 %copy-start.42 = (f32[320]{0:T(512)S(1)}, f32[320]{0:T(512)}, u32[]{:S(2)}) copy-start(f32[320]{0:T(512)} %param.27) | copy-start | bytes 3844
  2191.2 226.2 %copy-start.4 = (f32[1024,320]{0,1:T(8,128)S(1)}, f32[1024,320]{0,1:T(8,128)}, u32[]{:S(2)}) copy-start(f32[1024,320]{0,1:T(8,128)} %get-tuple-element.224) | copy-start | bytes 3932164
  2191.2 226.1 %copy-start.16 = (bf16[1,1024,320]{1,2,0:T(8,128)(2,1)S(1)}, bf16[1,1024,320]{1,2,0:T(8,128)(2,1)}, u32[]{:S(2)}) copy-start(bf16[1,1024,320]{1,2,0:T(8,128)(2,1)} %param.37) | copy-start | bytes 1966084
  2191.2 226.1 %copy-start.27 = (f32[1024]{0:T(1024)S(1)}, f32[1024]{0:T(1024)}, u32[]{:S(2)}) copy-start(f32[1024]{0:T(1024)} %copy-done.26) | copy-start | bytes 12292
  2191.2 226.1 %copy-start.29 = (f32[1024]{0:T(1024)S(1)}, f32[1024]{0:T(1024)}, u32[]{:S(2)}) copy-start(f32[1024]{0:T(1024)} %copy-done.28) | copy-start | bytes 12292
  2191.2 226.1 %copy-start.35 = (f32[1024]{0:T(1024)S(1)}, f32[1024]{0:T(1024)}, u32[]{:S(2)}) copy-start(f32[1024]{0:T(1024)} %copy-done.34) | copy-start | bytes 12292
  2191.2 226.1 %copy-start.37 = (f32[1024]{0:T(1024)S(1)}, f32[1024]{0:T(1024)}, u32[]{:S(2)}) copy-start(f32[1024]{0:T(1024)} %copy-done.36) | copy-start | bytes 12292
  2191.2 226.1 %copy-start.39 = (f32[320]{0:T(512)S(1)}, f32[320]{0:T(512)}, u32[]{:S(2)}) copy-start(f32[320]{0:T(512)} %param.29) | copy-start | bytes 3844
  2191.3 226.1 %copy-start.48 = (f32[320]{0:T(512)S(1)}, f32[320]{0:T(512)}, u32[]{:S(2)}) copy-start(f32[320]{0:T(512)} %param.34) | copy-start | bytes 3844
  2231.5 318.2 %copy-start.1 = (bf16[320,1280]{1,0:T(8,128)(2,1)S(1)}, bf16[320,1280]{1,0:T(8,128)(2,1)}, u32[]{:S(2)}) copy-start(bf16[320,1280]{1,0:T(8,128)(2,1)} %param.31) | copy-start | bytes 2457604
  2232.7 189.0 %copy-start.43 = (f32[320]{0:T(512)S(1)}, f32[320]{0:T(512)}, u32[]{:S(2)}) copy-start(f32[320]{0:T(512)} %get-tuple-element.142) | copy-start | bytes 3844
  2232.7 189.0 %copy-start.44 = (f32[320]{0:T(512)S(1)}, f32[320]{0:T(512)}, u32[]{:S(2)}) copy-start(f32[320]{0:T(512)} %get-tuple-element.148) | copy-start | bytes 3844
  (41 other events, 1254.4 us)
Sparse Core Ops, SparseCore 0:
  76.3 121.0 reduce-scatter.9
  203.1 40.4 all-gather.5
  554.9 25.5 all-gather.7
  586.2 131.5 reduce-scatter.11
  720.3 152.4 reduce-scatter.17
  875.4 153.1 reduce-scatter.13
  1044.0 70.1 all-gather.11
  1126.9 93.7 reduce-scatter.19
  1290.2 52.1 reduce-scatter.21
  1928.9 85.2 reduce-scatter.23
  2015.8 70.1 all-gather.9
  2087.6 55.3 all-gather.13
  2149.9 74.9 all-reduce.12
  2227.1 93.7 reduce-scatter.25
  2323.0 94.2 reduce-scatter.15
  2423.4 123.4 all-reduce.10
